TPU v7x, 256 devices: a whole 4x4x8 slice. The times are simulated.
256 devices in a mesh: seq: 2 (over z_lo), shard: 128 (over x, z_hi, y, core).
Axes of the slice: x: 4, y: 4, z: 8 (z_hi: 4, z_lo: 2; z = z_hi * 2 + z_lo), core: 2. Of those that a mesh axis runs over, the one named last changes fastest.
Arguments:
- tokens: bfloat16 [65536, 768], P(('shard', 'seq')), may hold values from -24 to 24
- w_qkv: bfloat16 [768, 2304], P('shard'), may hold values from -0.3125 to 0.3125
- bias_q: bfloat16 [768], P('shard'), may hold values from -1.1953125 to 1.1953125
- bias_v: bfloat16 [768], P('shard'), may hold values from -1.1953125 to 1.1953125
- w_out: bfloat16 [768, 768], P('shard'), may hold values from -0.4375 to 0.4375
- bias_out: bfloat16 [768], P('shard'), may hold values from -1.1953125 to 1.1953125
- gain_one: bfloat16 [768], P('shard'), may hold values from 0.5 to 1.5
- shift_one: bfloat16 [768], P('shard'), may hold values from -1.1953125 to 1.1953125
- w_in: bfloat16 [768, 3072], P('shard'), may hold values from -0.21875 to 0.21875
- bias_in: bfloat16 [3072], P('shard'), may hold values from -1.1953125 to 1.1953125
- w_down: bfloat16 [3072, 768], P('shard'), may hold values from -0.15625 to 0.15625
- bias_down: bfloat16 [768], P('shard'), may hold values from -1.1953125 to 1.1953125
- gain_two: bfloat16 [768], P('shard'), may hold values from 0.5 to 1.5
- shift_two: bfloat16 [768], P('shard'), may hold values from -1.1953125 to 1.1953125
- doc_lengths: int32 [128], replicated, may hold values from 1 to 1024, 65536 in all
- cotangent: bfloat16 [65536, 768], P(('shard', 'seq')), may hold values from -6 to 6
Outputs:
- layer_out: bfloat16 [65536, 768], P(('shard', 'seq'))
- grad_tokens: float32 [65536, 768], P(('shard', 'seq'))
- grad_w_qkv: float32 [768, 2304], P('shard')
- grad_bias_q: float32 [768], P('shard')
- grad_bias_v: float32 [768], P('shard')
- grad_w_out: float32 [768, 768], P('shard')
- grad_bias_out: float32 [768], P('shard')
- grad_gain_one: float32 [768], P('shard')
- grad_shift_one: float32 [768], P('shard')
- grad_w_in: float32 [768, 3072], P('shard')
- grad_bias_in: float32 [3072], P('shard')
- grad_w_down: float32 [3072, 768], P('shard')
- grad_bias_down: float32 [768], P('shard')
- grad_gain_two: float32 [768], P('shard')
- grad_shift_two: float32 [768], P('shard')
Inputs may be any that keep to these rules, and one draw needn't show every extreme that they name: `doc_lengths`: document lengths in stream order; the documents fill the 65536 tokens end to end, and the longest has exactly 1024 tokens.
All inputs are finite; a program needn't handle non-finite values.
Results may differ from a plain program's by a relative error of at most 0.025.
Values may be sent and summed in bfloat16 or wider, within the bound.
A program may use at most 192 MiB of HBM per device.

v0:
```python
import functools
import jax
import jax.numpy as jnp
from jax import lax
from jax.experimental import pallas as pl
from jax.experimental.pallas import tpu as pltpu
from jax.sharding import PartitionSpec as P

HEAD_DIM = 64
NORM_EPS = 1e-12
MESH = pl.DeviceIdType.MESH
ANY_SPACE = pl.BlockSpec(memory_space=pl.ANY)
IN_VMEM = pl.BlockSpec(memory_space=pltpu.VMEM)
LOG2E = 1.4426950408889634
TILE = 256
HALF = 384
BOTTOM = -1e30
EXTENT = {"x": 4, "y": 4, "z": 8}
ORDERS = (("z", "y", "x"), ("z", "y", "x"), ("z", "x", "y"))
X_FIRST, Y_FIRST = ("x", "y", "z"), ("y", "x", "z")
SUM_ORDERS = ((X_FIRST, X_FIRST, Y_FIRST), (X_FIRST, Y_FIRST, X_FIRST), (X_FIRST, X_FIRST, Y_FIRST))
OTHERS = {dim: range(1, size) for dim, size in EXTENT.items()}
HALVES = (((0, 256), (256, 128)), ((0, 128), (128, 256)), ((0, 256), (256, 128)))
STREAMS = (0, 1, 2)
WIDE = (2, 2, 4, 4, 2, 3, 8, HALF)
TALL = (4, 4, 2, 2, 2, 3, 8, HALF)


def place():
    s = lax.axis_index("shard")
    q = lax.axis_index("seq")
    return {
        "c": lax.rem(s, 2),
        "y": lax.rem(s // 2, 4),
        "x": s // 32,
        "z": lax.rem(s // 8, 4) * 2 + q,
    }


def device_at(at):
    return {
        "shard": ((at["x"] * 4 + at["z"] // 2) * 4 + at["y"]) * 2 + at["c"],
        "seq": lax.rem(at["z"], 2),
    }


def moved(at, **steps):
    new = dict(at)
    for dim, step in steps.items():
        size = 2 if dim == "c" else EXTENT[dim]
        new[dim] = lax.rem(at[dim] + step + size, size)
    return new


def stream_mates():
    s = lax.axis_index("shard")
    q = lax.axis_index("seq")
    partner = {"shard": s, "seq": 1 - q}
    after = {"shard": lax.rem(s + 2, 128), "seq": q}
    before = {"shard": lax.rem(s + 126, 128), "seq": q}
    return partner, before, after


def greet(targets):
    barrier = pltpu.get_barrier_semaphore()
    for target in targets:
        pl.semaphore_signal(barrier, inc=1, device_id=target, device_id_type=MESH)
    pl.semaphore_wait(barrier, len(targets))


def sending(src, dst, send, recv, target):
    return pltpu.make_async_remote_copy(
        src_ref=src, dst_ref=dst, send_sem=send, recv_sem=recv, device_id=target, device_id_type=MESH
    )


def neighbours(at):
    return [moved(at, **{d: step}) for d in ("x", "y", "z") for step in (1, -1)]


def octet_mates(me):
    across = dict(me)
    across["y"] = me["y"] + 1 - 2 * lax.rem(me["y"], 2)
    twin = moved(me, c=1)
    diagonal = dict(across)
    diagonal["c"] = twin["c"]
    return twin, across, diagonal


def span(index):
    return slice(None) if index is None else pl.ds(index, 1)


def picks_of(sets, gone=()):
    x, y, z = sets["x"], sets["y"], sets["z"]
    pick = {
        "x": x,
        "m": None if y is None else y // 2,
        "yp": None if y is None else lax.rem(y, 2),
        "zh": None if z is None else z // 2,
        "q": None if z is None else lax.rem(z, 2),
    }
    names = {"x": ("x",), "y": ("m", "yp"), "z": ("zh", "q")}
    for dim in gone:
        for name in names[dim]:
            pick[name] = 0
    return pick


WIDE_DIMS = ("yp", "q", "x", "zh", "m")
TALL_DIMS = ("x", "zh", "m", "yp", "q")
DIM_SIZE = {"yp": 2, "q": 2, "x": 4, "zh": 4, "m": 2}


def dims_of(k):
    return TALL_DIMS if k == 2 else WIDE_DIMS


def view(ref, k, part, sets, half=None, gone=(), lead=()):
    pick = picks_of(sets, gone)
    cut = (0, HALF) if half is None else HALVES[k][half]
    at = tuple(span(pick[d]) for d in dims_of(k))
    rows = () if part is None else (part,)
    return ref.at[(*lead, *at, *rows, slice(None), pl.ds(*cut))]


def find_docs(lengths, q_docs, k_docs):
    shard, seq = lax.axis_index("shard"), lax.axis_index("seq")
    stream_len = 128 * 2 * TILE
    row = lax.broadcasted_iota(jnp.int32, (128, 128), 0)
    column = lax.broadcasted_iota(jnp.int32, (128, 128), 1)
    wide = jnp.broadcast_to(lengths[...], (128, 128))
    starts_down = jnp.sum(jnp.where(column < row, wide, 0), axis=1, keepdims=True)
    lengths_down = jnp.sum(jnp.where(column == row, wide, 0), axis=1, keepdims=True)
    starts_across = jnp.sum(jnp.where(row < column, jnp.broadcast_to(lengths_down, (128, 128)), 0), axis=0, keepdims=True)
    origin = (shard // 2 - 1) * (4 * TILE)

    def tile(t, carry):
        at = origin + t * TILE + lax.broadcasted_iota(jnp.int32, (TILE, 1), 0)
        counted = jnp.sum((at >= starts_across).astype(jnp.int32), axis=1, keepdims=True) - 1
        k_docs[t] = jnp.where(at < stream_len, counted, stream_len)
        return carry

    lax.fori_loop(0, 12, tile, 0)
    for i in range(2):
        at = origin + (4 + seq + 2 * i) * TILE + lax.broadcasted_iota(jnp.int32, (1, TILE), 1)
        q_docs[i] = jnp.sum((starts_down <= at).astype(jnp.int32), axis=0, keepdims=True) - 1


def front_kernel(
    lengths, cat_ref, down_ref, vec_ref, tok_ref,
    first, second, third, rows_out, bias_in_out, window_out, kv_out, q_heads, o_heads, lse, attended,
    q_docs, k_docs,    land, stage, own, vecs, window, kv, w_heads, w_flat, top, total, acc,
    oct_s, oct_r, local, near_s, near_r, send, recv, core_s, core_r, vec_s, vec_r, tok_s, tok_r, keep, att_s, att_r,
):
    me = place()
    c, x, y, z = me["c"], me["x"], me["y"], me["z"]
    yp, q, m, zh = lax.rem(y, 2), lax.rem(z, 2), y // 2, z // 2
    outs = (first, second, third)
    twin, across, diagonal = octet_mates(me)
    twin_id = device_at(twin)
    partner, before, after = stream_mates()
    lines = [moved(me, **{d: o}) for d in EXTENT for o in OTHERS[d]]
    greet([device_at(a) for a in lines + [twin, diagonal]] + [before, after])

    def chunk_of(at):
        cols = (lax.rem(at["y"], 2) * 2 + q) * 768 + at["c"] * HALF
        return cat_ref.at[:, :, pl.ds(pl.multiple_of(cols, 128), HALF)]

    index = yp * 2 + c
    mates = (twin, across, diagonal)
    out = [
        sending(chunk_of(mate), land.at[:, index], oct_s.at[k], oct_r.at[k], device_at(mate))
        for k, mate in enumerate(mates)
    ]
    for cp in out:
        cp.start()
    kept = pltpu.make_async_copy(chunk_of(me), land.at[:, index], local.at[0])
    kept.start()
    gives = q == c
    down_out = sending(
        down_ref.at[:, :, pl.ds(pl.multiple_of((1 - c) * HALF, 128), HALF)], own.at[2], oct_s.at[3], oct_r.at[3], twin_id
    )
    down_kept = pltpu.make_async_copy(
        down_ref.at[:, :, pl.ds(pl.multiple_of(c * HALF, 128), HALF)], own.at[2], local.at[1]
    )

    @pl.when(gives)
    def _():
        down_out.start()
        down_kept.start()

    vec_kept = pltpu.make_async_copy(vec_ref, vecs.at[c, x, zh, y], local.at[2])
    vec_kept.start()

    sent = []

    def go(src, dst, send_sem, recv_sem, target):
        cp = sending(src, dst, send_sem, recv_sem, target)
        cp.start()
        sent.append(cp)

    def arrive(dst, send_sem, recv_sem, target):
        sending(dst, dst, send_sem, recv_sem, target).wait_recv()

    def tok_go(src, dst, at, target):
        go(src, dst, tok_s.at[at], tok_r.at[at], target)

    tok_kept = pltpu.make_async_copy(tok_ref, window.at[1, c, q], local.at[3])

    def tok_start():
        tok_kept.start()
        tok_go(tok_ref, window.at[1, c, q], 0, partner)
        tok_go(tok_ref, window.at[0, c, q], 1, after)
        tok_go(tok_ref, window.at[2, c, q], 2, before)
        tok_go(tok_ref, window.at[1, c, q], 3, twin_id)

    def tok_forward():
        theirs = window.at[1, c, 1 - q]
        arrive(theirs, tok_s.at[0], tok_r.at[0], partner)
        tok_go(theirs, window.at[0, c, 1 - q], 4, after)
        tok_go(theirs, window.at[2, c, 1 - q], 5, before)
        tok_go(theirs, window.at[1, c, 1 - q], 6, twin_id)

    def tok_share(h, first_slot, at):
        arrive(window.at[0, c, h], tok_s.at[first_slot], tok_r.at[first_slot], before)
        arrive(window.at[2, c, h], tok_s.at[first_slot + 1], tok_r.at[first_slot + 1], after)
        tok_go(window.at[0, c, h], window.at[0, c, h], at, twin_id)
        tok_go(window.at[2, c, h], window.at[2, c, h], at + 1, twin_id)

    vec_rounds = (("x", (1, 2, 3)), ("y", (1, 2, 3)), ("z", (2, 4, 6)), ("c", (1,)))

    def vec_copies(number, arriving):
        dim, steps = vec_rounds[number]
        done = [d for d, _ in vec_rounds[:number]]
        copies = []
        for k, step in enumerate(steps):
            source = moved(me, **{dim: (1 if dim == "c" else -step)}) if arriving else me
            pick = [None if d in done else (source["z"] // 2 if d == "z" else source[d]) for d in ("c", "x", "z", "y")]
            ref = vecs.at[tuple(span(p) for p in pick)]
            copies.append(
                sending(ref, ref, vec_s.at[number, k], vec_r.at[number, k], device_at(moved(me, **{dim: step})))
            )
        return copies

    def vec_start(number):
        for cp in vec_copies(number, False):
            cp.start()
            sent.append(cp)

    def vec_wait(number):
        for cp in vec_copies(number, True):
            cp.wait_recv()

    kept.wait()
    for k, mate in enumerate(mates):
        mate_index = lax.rem(mate["y"], 2) * 2 + mate["c"]
        arrive(land.at[:, mate_index], oct_s.at[k], oct_r.at[k], device_at(mate))
    for k in range(2):
        for owner in range(4):
            stage[pl.ds(6 * owner, 6), :] = land[k, owner].astype(jnp.float32)
        for part in range(3):
            own[k, part] = stage[pl.ds(8 * part, 8), :].astype(jnp.bfloat16)

    @pl.when(gives)
    def _():
        down_kept.wait()

    @pl.when(jnp.logical_not(gives))
    def _():
        down_out.wait_recv()

    homes = (first.at[c, yp, q, x, zh, m], second.at[c, yp, q, x, zh, m], third.at[c, x, zh, m, yp, q])
    flush = [pltpu.make_async_copy(own.at[k], homes[k], local.at[4 + k]) for k in STREAMS]
    for cp in flush:
        cp.start()
    twins = []

    def share(k, part, sets, half, slot):
        mine = view(outs[k], k, part, sets, half, (), (c,))
        theirs = view(outs[k], k, part, sets, half, (), (1 - c,))
        go(mine, mine, core_s.at[slot, k], core_r.at[slot, k], twin_id)
        twins.append((theirs, core_s.at[slot, k], core_r.at[slot, k]))

    def sets_at(part, phase, index):
        sets = {"x": x, "y": y, "z": z}
        for earlier in ORDERS[part][:phase]:
            sets[earlier] = None
        dim = ORDERS[part][phase]
        sets[dim] = lax.rem(index + EXTENT[dim], EXTENT[dim])
        return sets

    def near(k, part, phase, arriving):
        dim = ORDERS[part][phase]
        for o in OTHERS[dim]:
            sems = near_s.at[part, phase, o, k], near_r.at[part, phase, o, k]
            target = device_at(moved(me, **{dim: o}))
            if arriving:
                arrive(view(outs[k], k, part, sets_at(part, phase, me[dim] - o), None, (), (c,)), *sems, target)
            elif phase == 0:
                go(own.at[k, part], homes[k].at[part], *sems, target)
            else:
                ref = view(outs[k], k, part, sets_at(part, phase, me[dim]), None, (), (c,))
                go(ref, ref, *sems, target)

    def ring(k, part, step, arriving):
        dim = ORDERS[part][2]
        size = EXTENT[dim]
        for direction, sign in enumerate((1, -1)):
            sets = sets_at(part, 2, me[dim] - sign * (step if arriving else step - 1))
            half = direction if step == size // 2 else None
            ref = view(outs[k], k, part, sets, half, (), (c,))
            slot = part * 2 + step - 1
            sems = send.at[slot, direction, k], recv.at[slot, direction, k]
            target = device_at(moved(me, **{dim: sign}))
            if arriving:
                arrive(ref, *sems, target)
            else:
                go(ref, ref, *sems, target)

    def ring_share(k, part, step):
        dim = ORDERS[part][2]
        for direction, sign in enumerate((1, -1)):
            half = direction if step == EXTENT[dim] // 2 else None
            share(k, part, sets_at(part, 2, me[dim] - sign * step), half, 3 + (part * 2 + step - 1) * 2 + direction)

    parts = range(3)
    late = [(k, part) for k in (1, 2) for part in parts]
    for part in parts:
        near(0, part, 0, False)
    vec_kept.wait()
    vec_start(0)
    for k, part in late:
        near(k, part, 0, False)
    find_docs(lengths, q_docs, k_docs)
    for cp in flush:
        cp.wait()
    for part in parts:
        near(0, part, 0, True)
        near(0, part, 1, False)
    tok_start()
    vec_wait(0)
    vec_start(1)
    for part in parts:
        near(0, part, 1, True)
        ring(0, part, 1, False)
    for k, part in late:
        near(k, part, 0, True)
        near(k, part, 1, False)
    vec_wait(1)
    vec_start(2)
    tok_forward()
    for part in parts:
        ring(0, part, 1, True)
        ring(0, part, 2, False)
    vec_wait(2)
    vec_start(3)
    for k, part in late:
        near(k, part, 1, True)
        ring(k, part, 1, False)
    for k, part in late:
        share(k, part, sets_at(part, 2, me[ORDERS[part][2]]), None, part)
    vec_wait(3)
    for v in range(8):
        rows_out[v : v + 1] = jnp.zeros((1, 768), jnp.float32)
    lane = lax.broadcasted_iota(jnp.int32, (128, HALF), 0)
    line = lax.broadcasted_iota(jnp.int32, (512, HALF), 0)
    values = [vecs[owner_core].reshape(512, 128).astype(jnp.bfloat16) for owner_core in range(2)]
    for h in range(2):
        column = h * HALF + lax.broadcasted_iota(jnp.int32, (1, HALF), 1)
        cols = slice(h * HALF, (h + 1) * HALF)
        for owner_core in range(2):
            place_in = lax.rem(column, 12) - 6 * owner_core
            picked = dot32(values[owner_core], jnp.logical_and(lane == place_in, lane < 6).astype(jnp.bfloat16))
            for v in range(8):
                rows_out[v : v + 1, cols] += row_sum(jnp.where(line == column // 12 * 8 + v, picked, 0.0))

    def hidden_row(m, carry):
        column = m * HALF + lax.broadcasted_iota(jnp.int32, (1, HALF), 1)
        total = jnp.zeros((1, HALF), jnp.float32)
        for owner_core in range(2):
            place_in = lax.rem(column, 48) - 24 * owner_core
            inside = jnp.logical_and(place_in >= 0, place_in < 24)
            picked = dot32(values[owner_core], jnp.logical_and(lane == place_in + 6, inside).astype(jnp.bfloat16))
            total = total + row_sum(jnp.where(line == column // 48 * 8, picked, 0.0))
        bias_in_out[m] = total
        return carry

    lax.fori_loop(0, 8, hidden_row, 0)
    for part in parts:
        ring(0, part, 2, True)
    load = pltpu.make_async_copy(first.at[c, pl.ds(0, 2), pl.ds(0, 2)], w_heads, keep.at[1])
    load.start()
    go(first.at[c, 1, 1], first.at[c, 1, 1], core_s.at[0, 0], core_r.at[0, 0], twin_id)
    twins.append((first.at[1 - c, 1, 1], core_s.at[0, 0], core_r.at[0, 0]))

    own_half = pl.ds(pl.multiple_of(c * HALF, 128), HALF)
    bias = [rows_out[v : v + 1, own_half] for v in range(2)]
    arrive(window.at[1, 1 - c, q], tok_s.at[3], tok_r.at[3], twin_id)
    arrive(window.at[1, 1 - c, 1 - q], tok_s.at[6], tok_r.at[6], twin_id)
    tok_kept.wait()
    load.wait()

    def project_group(group):
        def one(n, carry):
            core, h = n // 2, lax.rem(n, 2)
            x_tile, t = window[group, core, h], group * 4 + n
            kv[0, t] = dot32(x_tile, weights(1)).astype(jnp.bfloat16)
            kv[1, t] = (dot32(x_tile, weights(2)) + bias[1]).astype(jnp.bfloat16)
            return carry

        lax.fori_loop(0, 4, one, 0)

    def flatten(i, carry):
        rows = pl.ds(pl.multiple_of(i * 192, 192), 192)
        for number in range(3):
            piece = w_heads[number // 2, number % 2, i].astype(jnp.float32)
            w_flat[number, rows] = piece.reshape(192, HALF).astype(jnp.bfloat16)
        return carry

    lax.fori_loop(0, 4, flatten, 0)

    def weights(number):
        return w_flat[number]

    low = lanes_low(TILE)
    scale = HEAD_DIM ** -0.5 * LOG2E

    def heads_front(pair, i, near_by):
        cols = slice(pair * 128, (pair + 1) * 128) if isinstance(pair, int) else pl.ds(pl.multiple_of(pair * 128, 128), 128)
        at = pair * 2 + i
        qs = q_heads[i, :, cols]
        none = jnp.zeros_like(qs)
        queries = (jnp.where(low, qs, none), jnp.where(low, none, qs))
        if near_by:
            top[at] = jnp.full((2, 1, TILE), BOTTOM, jnp.float32)
            total[at] = jnp.zeros((2, 1, TILE), jnp.float32)
            acc[at] = jnp.zeros((128, TILE), jnp.float32)

        def step(n, carry):
            u = q + 2 * i + n
            t = 4 + n if near_by else u + 4 * (u // 4)
            k, v = kv[0, t, :, cols], flipped(kv[1, t, :, cols])
            same = q_docs[i] == k_docs[t]
            scores = [jnp.where(same, across_lanes(k, queries[head]) * scale, BOTTOM) for head in range(2)]
            old = [top[at, head] for head in range(2)]
            new = [jnp.maximum(old[head], jnp.max(scores[head], axis=0, keepdims=True)) for head in range(2)]
            fade = [jnp.exp2(old[head] - new[head]) for head in range(2)]
            p = [jnp.exp2(scores[head] - new[head]) for head in range(2)]
            sums = [total[at, head] * fade[head] + jnp.sum(p[head], axis=0, keepdims=True) for head in range(2)]
            adds = [dot32(v[head * HEAD_DIM : (head + 1) * HEAD_DIM], p[head].astype(jnp.bfloat16)) for head in range(2)]
            for head in range(2):
                rows = slice(head * HEAD_DIM, (head + 1) * HEAD_DIM)
                acc[at, rows] = acc[at, rows] * fade[head] + adds[head]
                total[at, head] = sums[head]
                top[at, head] = new[head]
            return carry

        lax.fori_loop(0, 4 if near_by else 5, step, 0)
        if not near_by:
            for head in range(2):
                rows = slice(head * HEAD_DIM, (head + 1) * HEAD_DIM)
                acc[at, rows] = acc[at, rows] / total[at, head]
                lse[pair, i, head : head + 1] = top[at, head] + jnp.log2(total[at, head])
            o_heads[i, :, cols] = flipped(acc[at]).astype(jnp.bfloat16)

    def all_pairs(i, near_by):
        lax.fori_loop(0, 3, lambda pair, carry: (heads_front(pair, i, near_by), carry)[1], 0)

    for i in range(2):
        q_heads[i] = (dot32(window[1, i, q], weights(0)) + bias[0]).astype(jnp.bfloat16)
    project_group(1)
    all_pairs(0, True)
    tok_share(q, 1, 7)
    all_pairs(1, True)
    tok_share(1 - q, 4, 9)
    for part in parts:
        ring(1, part, 1, True)
        ring(1, part, 2, False)
    for h, at in ((q, 7), (1 - q, 9)):
        arrive(window.at[0, 1 - c, h], tok_s.at[at], tok_r.at[at], twin_id)
        arrive(window.at[2, 1 - c, h], tok_s.at[at + 1], tok_r.at[at + 1], twin_id)
    kept_window = pltpu.make_async_copy(window, window_out, keep.at[2])
    kept_window.start()
    project_group(0)
    for part in parts:
        ring(2, part, 1, True)
        ring(2, part, 2, False)
    project_group(2)
    kept_kv = pltpu.make_async_copy(kv, kv_out, keep.at[3])
    kept_kv.start()
    for part in parts:
        ring_share(1, part, 1)
    heads_front(0, 0, False)
    heads_front(1, 0, False)
    for part in parts:
        ring_share(2, part, 1)
    heads_front(2, 0, False)
    for part in parts:
        ring(1, part, 2, True)
        ring_share(1, part, 2)
    all_pairs(1, False)
    mine_cols, other_cols = (pl.ds(pl.multiple_of(a * HALF, 128), HALF) for a in (c, 1 - c))
    go(o_heads.at[1 - c], attended.at[:, mine_cols], att_s.at[0], att_r.at[0], twin_id)
    kept_att = pltpu.make_async_copy(o_heads.at[c], attended.at[:, mine_cols], keep.at[4])
    kept_att.start()
    for part in parts:
        ring(2, part, 2, True)
        ring_share(2, part, 2)
    for ref, send_sem, recv_sem in twins:
        arrive(ref, send_sem, recv_sem, twin_id)
    arrive(attended.at[:, other_cols], att_s.at[0], att_r.at[0], twin_id)
    for cp in (kept_window, kept_kv, kept_att):
        cp.wait()
    for cp in out + sent:
        cp.wait_send()

    @pl.when(gives)
    def _():
        down_out.wait_send()


def front(lengths, cat, down, vec, tokens):
    bf, f32, dma = jnp.bfloat16, jnp.float32, pltpu.SemaphoreType.DMA
    return pl.pallas_call(
        front_kernel,
        name="front",
        out_shape=(
            jax.ShapeDtypeStruct((2, *WIDE), bf),
            jax.ShapeDtypeStruct((2, *WIDE), bf),
            jax.ShapeDtypeStruct((2, *TALL), bf),
            jax.ShapeDtypeStruct((8, 768), f32),
            jax.ShapeDtypeStruct((8, 1, HALF), f32),
            jax.ShapeDtypeStruct((3, 2, 2, TILE, 768), bf),
            jax.ShapeDtypeStruct((2, 12, TILE, HALF), bf),
            jax.ShapeDtypeStruct((2, TILE, HALF), bf),
            jax.ShapeDtypeStruct((2, TILE, HALF), bf),
            jax.ShapeDtypeStruct((3, 2, 2, TILE), f32),
            jax.ShapeDtypeStruct((TILE, 768), bf),
        ),
        in_specs=[IN_VMEM] + [ANY_SPACE] * 4,
        out_specs=(ANY_SPACE,) * 3 + (IN_VMEM,) * 2 + (ANY_SPACE,) * 2 + (IN_VMEM,) * 4,
        scratch_shapes=[
            pltpu.VMEM((2, 1, TILE), jnp.int32),
            pltpu.VMEM((12, TILE, 1), jnp.int32),
            pltpu.VMEM((2, 4, 6, HALF), bf),
            pltpu.VMEM((24, HALF), f32),
            pltpu.VMEM((3, 3, 8, HALF), bf),
            pltpu.VMEM((2, 4, 4, 4, 8, 128), f32),
            pltpu.VMEM((3, 2, 2, TILE, 768), bf),
            pltpu.VMEM((2, 12, TILE, HALF), bf),
            pltpu.VMEM((2, 2, 4, 4, 2, 3, 8, HALF), bf),
            pltpu.VMEM((3, 768, HALF), bf),
            pltpu.VMEM((6, 2, 1, TILE), f32),
            pltpu.VMEM((6, 2, 1, TILE), f32),
            pltpu.VMEM((6, 128, TILE), f32),
            dma((4,)), dma((4,)), dma((7,)), dma((3, 2, 8, 3)), dma((3, 2, 8, 3)), dma((6, 2, 3)), dma((6, 2, 3)),
            dma((15, 3)), dma((15, 3)), dma((4, 3)), dma((4, 3)), dma((11,)), dma((11,)), dma((5,)), dma((1,)), dma((1,)),
        ],
        compiler_params=pltpu.CompilerParams(collective_id=1, has_side_effects=True, vmem_limit_bytes=62 << 20),
    )(lengths, cat, down, vec, tokens)


def back_kernel(*refs):
    (lengths, q_ref, o_ref, lse_ref, gv, d_att, kv_hbm, window_hbm, first, dwo, g1, g2, base) = refs[:13]
    (out0, out1, out2, out_v, out_tok) = refs[13:18]
    grads = (None, g1, g2)
    refs = refs[18:]
    acc, other, refs = refs[:3], refs[3:6], refs[6:]
    lands = {}
    for n, (part, phase, k) in enumerate((a, b, k) for a in range(3) for b in range(3) for k in STREAMS):
        lands[part, phase, k] = refs[n]
    refs = refs[27:]
    (
        stage, rows, tall_f, v_c, v_x, v_y, v_z, t_all, t_in, t_land, t_part, t_mate, t_base,
        kv, window, w_heads, dkv_all, dkv, dq_all, dq_acc, dw, q_rows, v_rows, q_docs, k_docs, do_ref,
        local, core_s, core_r, near_s, near_r, send, recv, fin_s, fin_r, t_s, t_r, vec_s, vec_r, tok_s, tok_r, tok_l, load, att_s, att_r,
    ) = refs
    me = place()
    c, x, y, z = me["c"], me["x"], me["y"], me["z"]
    yp, q, m, zh = lax.rem(y, 2), lax.rem(z, 2), y // 2, z // 2
    twin, across, diagonal = octet_mates(me)
    twin_id = device_at(twin)
    partner, before, after = stream_mates()

    def other_q(at):
        new = dict(at)
        new["z"] = at["z"] + 1 - 2 * lax.rem(at["z"], 2)
        return new

    ring_mates = [moved(me, **{d: k}) for d in ("x", "y", "z") for k in range(1, EXTENT[d])]
    mates = [twin, across, diagonal] + [other_q(a) for a in (me, twin, across, diagonal)]
    targets = ring_mates + [twin, diagonal] + [other_q(a) for a in (twin, across, diagonal)]
    greet([device_at(a) for a in targets] + [before, after])
    sent = []

    def go(src, dst, send_sem, recv_sem, target):
        cp = sending(src, dst, send_sem, recv_sem, target)
        cp.start()
        sent.append(cp)

    def arrive(dst, send_sem, recv_sem, target):
        sending(dst, dst, send_sem, recv_sem, target).wait_recv()

    def sets_of(k, part, phase, index):
        sets = {"x": x, "y": y, "z": z}
        order = SUM_ORDERS[k][part]
        for later in order[phase + 1:]:
            sets[later] = None
        sets[order[phase]] = lax.rem(index + 2 * EXTENT[order[phase]], EXTENT[order[phase]])
        return sets

    def add_region(k, part, sets, sources, half=None, gone=()):
        pick, from_pick = picks_of(sets), picks_of(sets, gone)
        dims = dims_of(k)
        inner = dims[3:] if k < 2 else dims[2:]
        outer = [d for d in dims if d not in inner and pick[d] is None]
        count = 1
        for d in outer:
            count *= DIM_SIZE[d]
        cut = pl.ds(*((0, HALF) if half is None else HALVES[k][half]))

        def one(i):
            at = {}
            for d in reversed(outer):
                at[d] = lax.rem(i, DIM_SIZE[d]) if count > 1 else 0
                i = i // DIM_SIZE[d]

            def index(picked):
                return tuple(
                    (at[d] if d in at else slice(None)) if picked[d] is None else pl.ds(picked[d], 1) if d in inner else picked[d]
                    for d in dims
                )

            to = (*index(pick), part, slice(None), cut)
            fr = (*index(from_pick), slice(None), cut)
            if len(sources) == 1:
                acc[k][to] = acc[k][to] + sources[0][fr]
            else:
                total = acc[k][to].astype(jnp.float32)
                for src in sources:
                    total = total + src[fr].astype(jnp.float32)
                acc[k][to] = total.astype(jnp.bfloat16)

        if count == 1:
            one(0)
        else:
            lax.fori_loop(0, count, lambda i, carry: (one(i), carry)[1], 0)

    def hop(k, part, n):
        return sets_of(k, part, 0, me[SUM_ORDERS[k][part][0]] + (2, 1, -1, 0)[n])

    own_copies = {}

    def cross(k, part, n):
        slot = part * 4 + n
        sets = hop(k, part, n)
        src = view(grads[k], k, part, sets, None, (), (1 - c,))
        go(src, view(other[k], k, part, sets), core_s.at[slot, k], core_r.at[slot, k], twin_id)
        kept = pltpu.make_async_copy(
            view(grads[k], k, part, sets, None, (), (c,)), view(acc[k], k, part, sets), local.at[slot, k]
        )
        kept.start()
        own_copies[k, part, n] = kept

    loads = [
        pltpu.make_async_copy(kv_hbm, kv, load.at[0]),
        pltpu.make_async_copy(first.at[c, pl.ds(0, 3)], w_heads, load.at[1]),
        pltpu.make_async_copy(window_hbm, window, load.at[2]),
        pltpu.make_async_copy(dwo.at[c], acc[0].at[1, 1], load.at[3]),
        pltpu.make_async_copy(base, t_base, load.at[4]),
    ]
    loads[0].start()
    own_half, other_half = (pl.ds(pl.multiple_of(a * HALF, 128), HALF) for a in (c, 1 - c))
    go(d_att.at[:, other_half], do_ref.at[c], att_s.at[0], att_r.at[0], twin_id)
    d_kept = pltpu.make_async_copy(d_att.at[:, own_half], do_ref.at[c], load.at[5])
    d_kept.start()
    for n in range(4):
        for k in (1, 2):
            for part in range(3):
                cross(k, part, n)

    for cp in loads[1:]:
        cp.start()
    go(dwo.at[1 - c], other[0], core_s.at[0, 0], core_r.at[0, 0], twin_id)

    vec_lands = (v_c, v_x, v_y, v_z)
    vec_dims = ("c", "x", "y", "z")

    def vec_start(number):
        dim, land = vec_dims[number], vec_lands[number]
        for k in range(1, land.shape[0]):
            mine = land.at[me[dim]]
            go(mine, mine, vec_s.at[number, k], vec_r.at[number, k], device_at(moved(me, **{dim: k})))

    def vec_finish(number):
        dim, land = vec_dims[number], vec_lands[number]
        size = land.shape[0]
        for k in range(1, size):
            theirs = land.at[lax.rem(me[dim] - k + size, size)]
            arrive(theirs, vec_s.at[number, k], vec_r.at[number, k], device_at(moved(me, **{dim: k})))
        total = land[0].astype(jnp.float32)
        for k in range(1, size):
            total = total + land[k].astype(jnp.float32)
        return total

    def row_blocks(fn):
        lax.fori_loop(0, TILE // 32, lambda r, carry: (fn(pl.ds(pl.multiple_of(r * 32, 32), 32)), carry)[1], 0)

    def tok_twin(group, at):
        go(t_all.at[1 - c, group], t_in.at[group], tok_s.at[at], tok_r.at[at], twin_id)

    def tok_edges():
        for n, (group, at) in enumerate(((0, 0), (2, 6))):
            arrive(t_in.at[group], tok_s.at[at], tok_r.at[at], twin_id)
        for n, h in enumerate((1 - q, q)):
            for group in (0, 2):
                def one(at):
                    t_all[c, group, h, at] = t_all[c, group, h, at] + t_in[group, h, at]
                row_blocks(one)
            go(t_all.at[c, 0, h], t_land.at[1, h], tok_s.at[1 + n], tok_r.at[1 + n], before)
            go(t_all.at[c, 2, h], t_land.at[0, h], tok_s.at[3 + n], tok_r.at[3 + n], after)

    def tok_total(h, at):
        f = jnp.float32
        return t_all[c, 1, h, at].astype(f) + t_in[1, h, at].astype(f) + t_land[0, h, at].astype(f) + t_land[1, h, at].astype(f)

    def tok_theirs():
        h = 1 - q
        arrive(t_in.at[1], tok_s.at[7], tok_r.at[7], twin_id)
        arrive(t_land.at[1, h], tok_s.at[1], tok_r.at[1], after)
        arrive(t_land.at[0, h], tok_s.at[3], tok_r.at[3], before)

        def one(at):
            t_part[at] = tok_total(h, at).astype(jnp.bfloat16)
        row_blocks(one)
        go(t_part, t_mate, tok_s.at[5], tok_r.at[5], partner)

    def tok_mine():
        arrive(t_land.at[1, q], tok_s.at[2], tok_r.at[2], after)
        arrive(t_land.at[0, q], tok_s.at[4], tok_r.at[4], before)
        arrive(t_mate, tok_s.at[5], tok_r.at[5], partner)
        loads[4].wait()

        def one(at):
            t_base[at] = tok_total(q, at) + t_mate[at].astype(jnp.float32) + t_base[at]
        row_blocks(one)
        done = pltpu.make_async_copy(t_base, out_tok, tok_l.at[0])
        done.start()
        return done

    def meet(k, part, n):
        slot = part * 4 + n
        own_copies[k, part, n].wait()
        sets = hop(k, part, n)
        arrive(view(other[k], k, part, sets), core_s.at[slot, k], core_r.at[slot, k], twin_id)
        add_region(k, part, sets, [other[k].at[(slice(None),) * 5 + (part,)]])

    def meet_out():
        loads[3].wait()
        arrive(other[0], core_s.at[0, 0], core_r.at[0, 0], twin_id)

        def one(i, carry):
            acc[0][1, 1, i] = acc[0][1, 1, i] + other[0][i]
            return carry

        lax.fori_loop(0, 4, one, 0)

    def ring(k, part, step, arriving):
        dim = SUM_ORDERS[k][part][0]
        ahead = 3 - step - (1 if arriving else 0)
        for direction, sign in enumerate((1, -1)):
            half = direction if step == 1 else None
            sets = sets_of(k, part, 0, me[dim] + sign * ahead)
            land = lands[part, 0, k].at[direction, step - 1]
            slot = part * 2 + step - 1
            sems = send.at[slot, direction, k], recv.at[slot, direction, k]
            target = device_at(moved(me, **{dim: sign}))
            here = view(land, k, None, sets, half, (dim,))
            if arriving:
                arrive(here, *sems, target)
                add_region(k, part, sets, [land], half, (dim,))
            else:
                go(view(acc[k], k, part, sets, half), here, *sems, target)

    def near(k, part, phase, arriving):
        order = SUM_ORDERS[k][part]
        dim, gone = order[phase], order[: phase + 1]
        mine = sets_of(k, part, phase, me[dim])
        sources = []
        for o in OTHERS[dim]:
            sems = near_s.at[part, phase - 1, o, k], near_r.at[part, phase - 1, o, k]
            target = device_at(moved(me, **{dim: o}))
            land = lands[part, phase, k].at[o - 1]
            here = view(land, k, None, mine, None, gone)
            if arriving:
                arrive(here, *sems, target)
                sources.append(land)
            else:
                go(view(acc[k], k, part, sets_of(k, part, phase, me[dim] + o)), here, *sems, target)
        if arriving:
            add_region(k, part, mine, sources, None, gone)

    def vec_next(n):
        total = vec_finish(n)
        if n < 3:
            vec_lands[n + 1][me[vec_dims[n + 1]]] = total.astype(jnp.bfloat16)
            vec_start(n + 1)
        else:
            out_v[...] = total

    low = lanes_low(TILE)
    scale = HEAD_DIM ** -0.5 * LOG2E
    picker = (
        lax.broadcasted_iota(jnp.int32, (8, 128), 0) == lax.broadcasted_iota(jnp.int32, (8, 128), 1) // HEAD_DIM
    ).astype(jnp.float32)

    def heads_back(pair, i, near_by):
        cols = slice(pair * 128, (pair + 1) * 128)
        place_at = pair * 2 + i
        qs, d_out = q_ref[i, :, cols], do_ref[i, :, cols]
        none = jnp.zeros_like(qs)
        q_heads = (jnp.where(low, qs, none), jnp.where(low, none, qs))
        do_heads = (jnp.where(low, d_out, none), jnp.where(low, none, d_out))
        prod = d_out.astype(jnp.float32) * o_ref[i, :, cols].astype(jnp.float32)
        deltas = lax.dot_general(
            picker, prod, (((1,), (1,)), ((), ())), precision=lax.Precision.HIGHEST, preferred_element_type=jnp.float32
        )
        if i == 0:
            dkv[...] = jnp.zeros_like(dkv)
        if not near_by:
            dq_acc[place_at] = jnp.zeros((128, TILE), jnp.float32)

        def step(n, carry):
            u = q + 2 * i + n
            t = 4 + n if near_by else u + 4 * (u // 4)
            slot = n if near_by else u
            k, v = kv[0, t, :, cols], kv[1, t, :, cols]
            k_flip = flipped(k)
            same = q_docs[i] == k_docs[t]
            heads = range(2)
            scores = [across_lanes(k, q_heads[h]) * scale for h in heads]
            dp = [across_lanes(v, do_heads[h]) for h in heads]
            p = [jnp.where(same, jnp.exp2(scores[h] - lse_ref[pair, i, h : h + 1]), 0.0) for h in heads]
            ds = [(p[h] * (dp[h] - deltas[h : h + 1])).astype(jnp.bfloat16) for h in heads]
            p_low = [p[h].astype(jnp.bfloat16) for h in heads]
            dq = [dot32(k_flip[h * HEAD_DIM : (h + 1) * HEAD_DIM], ds[h]) for h in heads]
            dk = [dot32(ds[h], q_heads[h]) for h in heads]
            dv = [dot32(p_low[h], do_heads[h]) for h in heads]
            for h in heads:
                lanes = slice(h * HEAD_DIM, (h + 1) * HEAD_DIM)
                dq_acc[place_at, lanes] = dq_acc[place_at, lanes] + dq[h]
            dkv[0, slot] = dkv[0, slot] + (dk[0] + dk[1])
            dkv[1, slot] = dkv[1, slot] + (dv[0] + dv[1])
            return carry

        lax.fori_loop(0, 4 if near_by else 5, step, 0)
        if near_by:
            dq_all[i, :, cols] = flipped(dq_acc[place_at] * HEAD_DIM ** -0.5).astype(jnp.bfloat16)
        if i == 1:
            def keep(u, carry):
                t = 4 + u if near_by else u + 4 * (u // 4)
                dkv_all[0, t, :, cols] = (dkv[0, u] * HEAD_DIM ** -0.5).astype(jnp.bfloat16)
                dkv_all[1, t, :, cols] = dkv[1, u].astype(jnp.bfloat16)
                return carry

            lax.fori_loop(0, 4 if near_by else 8, keep, 0)

    def tile_back(group, n):
        core, h = n // 2, lax.rem(n, 2)
        t = group * 4 + n
        x_flip = flipped(window[t])
        dk, dv = dkv_all[0, t], dkv_all[1, t]
        dw[1] += dot32(x_flip, dk)
        dw[2] += dot32(x_flip, dv)
        v_rows[...] = v_rows[...] + jnp.sum(dv.astype(jnp.float32), axis=0, keepdims=True)
        dx = across_lanes(dk, w_heads[1]) + across_lanes(dv, w_heads[2])
        t_all[core, group, h] = dx.astype(jnp.bfloat16)
        if group == 1:
            @pl.when(h == q)
            def _():
                dq = dq_all[core]
                dw[0] += dot32(x_flip, dq)
                q_rows[...] = q_rows[...] + jnp.sum(dq.astype(jnp.float32), axis=0, keepdims=True)
                t_all[core, group, h] = (dx + across_lanes(dq, w_heads[0])).astype(jnp.bfloat16)

    def tiles_back(group):
        lax.fori_loop(0, 4, lambda n, carry: (tile_back(group, n), carry)[1], 0)

    parts = range(3)
    late = [(k, part) for k in (1, 2) for part in parts]
    find_docs(lengths, q_docs, k_docs)
    for k, part in late:
        meet(k, part, 0)
        ring(k, part, 1, False)
    loads[0].wait()
    d_kept.wait()
    arrive(do_ref.at[1 - c], att_s.at[0], att_r.at[0], twin_id)
    heads_back(0, 0, False)
    for k, part in late:
        meet(k, part, 1)
        meet(k, part, 2)
    for part in parts:
        ring(1, part, 1, True)
        ring(1, part, 2, False)
    heads_back(0, 1, False)
    for part in parts:
        ring(2, part, 1, True)
        ring(2, part, 2, False)
    heads_back(1, 0, False)
    for k, part in late:
        meet(k, part, 3)
    meet_out()
    heads_back(1, 1, False)
    heads_back(2, 0, False)
    for part in parts:
        ring(1, part, 2, True)
        near(1, part, 1, False)
    heads_back(2, 1, False)
    loads[1].wait()
    loads[2].wait()
    dw[...] = jnp.zeros_like(dw)
    q_rows[...] = jnp.zeros_like(q_rows)
    v_rows[...] = jnp.zeros_like(v_rows)
    tiles_back(0)
    tok_twin(0, 0)
    tiles_back(2)
    tok_twin(2, 6)
    for part in parts:
        ring(2, part, 2, True)
        near(2, part, 1, False)
    heads_back(0, 0, True)
    heads_back(0, 1, True)
    for part in parts:
        near(1, part, 1, True)
        near(1, part, 2, False)
    heads_back(1, 0, True)
    heads_back(1, 1, True)
    for part in parts:
        near(2, part, 1, True)
        near(2, part, 2, False)
    heads_back(2, 0, True)
    heads_back(2, 1, True)
    for k, part in late:
        near(k, part, 2, True)
    tok_edges()
    tiles_back(1)
    tok_twin(1, 7)

    def grads_low(i, carry):
        rows_at = pl.ds(pl.multiple_of(i * 192, 192), 192)
        for number, (a, b) in enumerate(((0, 0), (0, 1), (1, 0))):
            acc[0][a, b, i] = dw[number, rows_at].reshape(4, 2, 3, 8, HALF).astype(jnp.bfloat16)
        return carry

    lax.fori_loop(0, 4, grads_low, 0)
    for part in parts:
        ring(0, part, 1, False)
    v_c[c] = gv[...]
    half_cols = pl.ds(pl.multiple_of(c * HALF, 128), HALF)
    v_c[c, 0:1, half_cols] = q_rows[...]
    v_c[c, 1:2, half_cols] = v_rows[...]
    vec_start(0)
    vec_next(0)
    for part in parts:
        ring(0, part, 1, True)
        ring(0, part, 2, False)
    vec_next(1)
    tok_theirs()
    for part in parts:
        ring(0, part, 2, True)
        near(0, part, 1, False)
    vec_next(2)
    for part in parts:
        near(0, part, 1, True)
        near(0, part, 2, False)
    vec_next(3)
    for part in parts:
        near(0, part, 2, True)

    for k in range(2):
        for part in range(3):
            stage[pl.ds(8 * part, 8), :] = acc[k][yp, q, x, zh, m, part].astype(jnp.float32)
        for owner in range(4):
            rows[k, owner] = stage[pl.ds(6 * owner, 6), :]
    for part in range(3):
        tall_f[part] = acc[2][x, zh, m, yp, q, part].astype(jnp.float32)

    def cols_at(at):
        return pl.ds(pl.multiple_of((lax.rem(at["y"], 2) * 2 + lax.rem(at["z"], 2)) * 768 + at["c"] * HALF, 128), HALF)

    def owner_of(at):
        return lax.rem(at["y"], 2) * 2 + at["c"]

    for k, out in enumerate((out0, out1)):
        for n, mate in enumerate(mates):
            go(rows.at[k, owner_of(mate)], out.at[:, cols_at(me)], fin_s.at[k, n], fin_r.at[k, n], device_at(mate))
    kept = [
        pltpu.make_async_copy(rows.at[k, owner_of(me)], out.at[:, cols_at(me)], fin_s.at[k, 7])
        for k, out in enumerate((out0, out1))
    ]
    for cp in kept:
        cp.start()
    stays = c == q
    half_at = [pl.ds(pl.multiple_of(a * HALF, 128), HALF) for a in (c, 1 - c)]
    t_self = pltpu.make_async_copy(tall_f, out2.at[:, :, half_at[0]], t_s.at[0])
    there_same, there_cross = device_at(other_q(me)), device_at(other_q(twin))
    t_twin = sending(tall_f, out2.at[:, :, half_at[0]], t_s.at[0], t_r.at[0], twin_id)
    t_same = sending(tall_f, out2.at[:, :, half_at[0]], t_s.at[1], t_r.at[1], there_same)
    t_cross = sending(tall_f, out2.at[:, :, half_at[0]], t_s.at[1], t_r.at[2], there_cross)

    @pl.when(stays)
    def _():
        t_self.start()
        t_same.start()

    @pl.when(jnp.logical_not(stays))
    def _():
        t_twin.start()
        t_cross.start()

    for k, out in enumerate((out0, out1)):
        for n, mate in enumerate(mates):
            arrive(out.at[:, cols_at(mate)], fin_s.at[k, n], fin_r.at[k, n], device_at(mate))

    @pl.when(stays)
    def _():
        arrive(out2.at[:, :, half_at[1]], t_s.at[0], t_r.at[0], twin_id)
        t_self.wait()
        t_same.wait_send()

    @pl.when(jnp.logical_not(stays))
    def _():
        arrive(out2.at[:, :, half_at[0]], t_s.at[1], t_r.at[1], there_same)
        arrive(out2.at[:, :, half_at[1]], t_s.at[1], t_r.at[2], there_cross)
        t_twin.wait_send()
        t_cross.wait_send()

    tok_mine().wait()
    for cp in kept:
        cp.wait()
    for cp in sent:
        cp.wait_send()


def back(lengths, q_heads, o_heads, lse, gv, d_att, kv, window, first, dwo, g1, g2, base):
    bf, f32, dma = jnp.bfloat16, jnp.float32, pltpu.SemaphoreType.DMA
    lands = []
    for part in range(3):
        for phase in range(3):
            for k in STREAMS:
                order = SUM_ORDERS[k][part]
                size = dict(DIM_SIZE)
                for dim, names in (("x", ("x",)), ("y", ("m", "yp")), ("z", ("zh", "q"))):
                    if dim in order[: phase + 1]:
                        for name in names:
                            size[name] = 1
                count = (2, 2) if phase == 0 else (EXTENT[order[phase]] - 1,)
                lands.append(pltpu.VMEM((*count, *(size[d] for d in dims_of(k)), 8, HALF), bf))
    whole = [pltpu.VMEM(WIDE, bf), pltpu.VMEM(TALL, bf)]
    return pl.pallas_call(
        back_kernel,
        name="back",
        out_shape=(
            jax.ShapeDtypeStruct((6, 3072), f32),
            jax.ShapeDtypeStruct((6, 3072), f32),
            jax.ShapeDtypeStruct((3, 8, 768), f32),
            jax.ShapeDtypeStruct((16, 768), f32),
            jax.ShapeDtypeStruct((TILE, 768), f32),
        ),
        in_specs=[IN_VMEM] * 5 + [ANY_SPACE] * 8,
        out_specs=(ANY_SPACE, ANY_SPACE, ANY_SPACE, IN_VMEM, ANY_SPACE),
        scratch_shapes=[
            pltpu.VMEM(WIDE, bf), *whole, pltpu.VMEM((4, 4, 2, 3, 8, HALF), bf), *whole, *lands,
            pltpu.VMEM((24, HALF), f32),
            pltpu.VMEM((2, 4, 6, HALF), f32),
            pltpu.VMEM((3, 8, HALF), f32),
            pltpu.VMEM((2, 16, 768), f32),
            pltpu.VMEM((4, 16, 768), bf),
            pltpu.VMEM((4, 16, 768), bf),
            pltpu.VMEM((8, 16, 768), bf),
            pltpu.VMEM((2, 3, 2, TILE, 768), bf),
            pltpu.VMEM((3, 2, TILE, 768), bf),
            pltpu.VMEM((2, 2, TILE, 768), bf),
            pltpu.VMEM((TILE, 768), bf),
            pltpu.VMEM((TILE, 768), bf),
            pltpu.VMEM((TILE, 768), f32),
            pltpu.VMEM((2, 12, TILE, HALF), bf),
            pltpu.VMEM((12, TILE, 768), bf),
            pltpu.VMEM((3, 768, HALF), bf),
            pltpu.VMEM((2, 12, TILE, HALF), bf),
            pltpu.VMEM((2, 8, TILE, 128), f32),
            pltpu.VMEM((2, TILE, HALF), bf),
            pltpu.VMEM((6, 128, TILE), f32),
            pltpu.VMEM((3, 768, HALF), f32),
            pltpu.VMEM((1, HALF), f32),
            pltpu.VMEM((1, HALF), f32),
            pltpu.VMEM((2, 1, TILE), jnp.int32),
            pltpu.VMEM((12, TILE, 1), jnp.int32),
            pltpu.VMEM((2, TILE, HALF), bf),
            dma((12, 3)), dma((12, 3)), dma((12, 3)), dma((3, 2, 8, 3)), dma((3, 2, 8, 3)), dma((6, 2, 3)), dma((6, 2, 3)),
            dma((2, 8)), dma((2, 7)),
            dma((2,)), dma((3,)), dma((4, 8)), dma((4, 8)), dma((8,)), dma((8,)), dma((1,)), dma((6,)), dma((1,)), dma((1,)),
        ],
        compiler_params=pltpu.CompilerParams(collective_id=2, has_side_effects=True, vmem_limit_bytes=63 << 20),
    )(lengths, q_heads, o_heads, lse, gv, d_att, kv, window, first, dwo, g1, g2, base)


def dot32(a, b):
    return jnp.dot(a, b, preferred_element_type=jnp.float32)


def lanes_low(rows):
    return lax.broadcasted_iota(jnp.int32, (rows, 128), 1) < HEAD_DIM


def across_lanes(a, b):
    return lax.dot_general(a, b, (((1,), (1,)), ((), ())), preferred_element_type=jnp.float32)


def flipped(a):
    return jnp.swapaxes(a, 0, 1)


def norm_parts(resid):
    centred = resid - jnp.mean(resid, axis=1, keepdims=True)
    inverse = lax.rsqrt(jnp.mean(centred * centred, axis=1, keepdims=True) + NORM_EPS)
    return centred * inverse, inverse


def norm_back(upstream, gain, n, inverse):
    e = upstream * gain
    return inverse * (e - jnp.mean(e, axis=1, keepdims=True) - n * jnp.mean(e * n, axis=1, keepdims=True))


def row_sum(a):
    return jnp.sum(a, axis=0, keepdims=True)


def mlp_kernel(
    att_ref, tok_ref, cot_ref, rows, bias_in, first, second, third,
    out_ref, d_one_ref, d_att_ref, dwo_ref, dw_in_ref, dw_down_ref, sums_ref,
    w_out, w_in, w_down, n_one, low, low_flip, slope, active, wide, sem,
):
    f32, bf = jnp.float32, jnp.bfloat16
    loads = [pltpu.make_async_copy(first.at[:, 3], w_out, sem.at[0])]
    loads += [pltpu.make_async_copy(second, w_in, sem.at[1]), pltpu.make_async_copy(third, w_down, sem.at[2])]
    for cp in loads:
        cp.start()

    def row(n):
        return rows[n : n + 1]

    halves = (slice(0, HALF), slice(HALF, 768))
    loads[0].wait()
    att = att_ref[...]
    for h in range(2):
        wide[:, halves[h]] = dot32(att, w_out[h])
    one, inverse_one = norm_parts(tok_ref[...].astype(f32) + (wide[...] + row(2)))
    n_one[...] = one
    normed = one * row(3) + row(4)
    low[...] = normed.astype(bf)
    low_flip[...] = flipped(low[...])
    wide[...] = normed + row(5)
    loads[1].wait()
    loads[2].wait()

    def up(m, carry):
        h = dot32(low[...], w_in[lax.rem(m, 2), m // 2]) + bias_in[m]
        cdf = 0.5 * (1.0 + lax.erf(h * 0.7071067811865476))
        slope[m] = cdf + h * jnp.exp(h * h * -0.5) * 0.3989422804014327
        a = (h * cdf).astype(bf)
        active[m] = flipped(a)
        for k in range(2):
            wide[:, halves[k]] += dot32(a, w_down[k, m])
        return carry

    lax.fori_loop(0, 8, up, 0)
    two, inverse_two = norm_parts(wide[...])
    out_ref[...] = (two * row(6) + row(7)).astype(bf)
    upstream = cot_ref[...].astype(f32)
    sums_ref[0:2] = jnp.zeros((2, 768), f32)
    sums_ref[12:16] = jnp.zeros((4, 768), f32)
    sums_ref[6:7] = row_sum(upstream * two)
    sums_ref[7:8] = row_sum(upstream)
    d_two = norm_back(upstream, row(6), two, inverse_two)
    sums_ref[5:6] = row_sum(d_two)
    d_low = d_two.astype(bf)
    wide[...] = d_two

    def down(m, carry):
        d_active = None
        for k in range(2):
            d_half = d_low[:, halves[k]]
            dw_down_ref[k, m] = dot32(active[m], d_half).astype(bf)
            part = across_lanes(d_half, w_down[k, m])
            d_active = part if d_active is None else d_active + part
        d_hidden = (d_active * slope[m]).astype(bf)
        sums_ref[pl.ds(8 + m // 2, 1), pl.ds(pl.multiple_of(lax.rem(m, 2) * HALF, 128), HALF)] = row_sum(d_hidden.astype(f32))
        dw_in_ref[lax.rem(m, 2), m // 2] = dot32(low_flip[...], d_hidden).astype(bf)
        wide[...] += across_lanes(d_hidden, w_in[lax.rem(m, 2), m // 2])
        return carry

    lax.fori_loop(0, 8, down, 0)
    d_normed = wide[...]
    one = n_one[...]
    sums_ref[3:4] = row_sum(d_normed * one)
    sums_ref[4:5] = row_sum(d_normed)
    d_one = norm_back(d_normed, row(3), one, inverse_one)
    d_one_ref[...] = d_one
    sums_ref[2:3] = row_sum(d_one)
    d_low = d_one.astype(bf)
    att_flip = flipped(att_ref[...])
    d_att = None
    for h in range(2):
        d_half = d_low[:, halves[h]]
        dwo_ref[h] = dot32(att_flip, d_half).astype(bf)
        part = across_lanes(d_half, w_out[h])
        d_att = part if d_att is None else d_att + part
    d_att_ref[...] = d_att.astype(bf)


def mlp(att, tokens, cotangent, rows, bias_in, first, second, third):
    f32, bf = jnp.float32, jnp.bfloat16
    return pl.pallas_call(
        mlp_kernel,
        name="mlp",
        in_specs=[IN_VMEM] * 5 + [ANY_SPACE] * 3,
        out_specs=(IN_VMEM,) * 7,
        out_shape=(
            jax.ShapeDtypeStruct((TILE, 768), bf),
            jax.ShapeDtypeStruct((TILE, 768), f32),
            jax.ShapeDtypeStruct((TILE, 768), bf),
            jax.ShapeDtypeStruct((2, 768, HALF), bf),
            jax.ShapeDtypeStruct((2, 4, 768, HALF), bf),
            jax.ShapeDtypeStruct((2, 8, HALF, HALF), bf),
            jax.ShapeDtypeStruct((16, 768), f32),
        ),
        scratch_shapes=[
            pltpu.VMEM((2, 768, HALF), bf),
            pltpu.VMEM((2, 4, 768, HALF), bf),
            pltpu.VMEM((2, 8, HALF, HALF), bf),
            pltpu.VMEM((TILE, 768), f32),
            pltpu.VMEM((TILE, 768), bf),
            pltpu.VMEM((768, TILE), bf),
            pltpu.VMEM((8, TILE, HALF), f32),
            pltpu.VMEM((8, HALF, TILE), bf),
            pltpu.VMEM((TILE, 768), f32),
            pltpu.SemaphoreType.DMA((3,)),
        ],
        compiler_params=pltpu.CompilerParams(vmem_limit_bytes=58 << 20),
    )(att, tokens, cotangent, rows, bias_in, first, second, third)


def body(
    tokens, w_qkv, bias_q, bias_v, w_out, bias_out, gain_one, shift_one, w_in, bias_in,
    w_down, bias_down, gain_two, shift_two, doc_lengths, cotangent,
):
    shard = lax.axis_index("shard")
    f32 = jnp.float32
    width = tokens.shape[1]

    vectors = (bias_q, bias_v, bias_out, gain_one, shift_one, bias_down, gain_two, shift_two)
    vec = jnp.concatenate(
        [
            jnp.stack(vectors).astype(f32),
            jnp.pad(bias_in.astype(f32).reshape(1, 24), ((0, 7), (0, 0))),
            jnp.zeros((8, 98), f32),
        ],
        axis=1,
    )
    cat = jnp.stack([jnp.concatenate([w_qkv, w_out], axis=1), w_in])
    lengths = doc_lengths.reshape(1, 128)
    first, second, third, rows, hidden_bias, window, kv, q_heads, o_heads, lse, attended = front(
        lengths, cat, w_down.reshape(3, 8, width), vec, tokens
    )
    first = first.reshape(2, 4, width, HALF)
    second = second.reshape(2, 4, width, HALF)
    third = third.reshape(2, 8, HALF, HALF)
    window = window.reshape(12, TILE, width)
    layer_out, d_one, d_att, dw_out, dw_in, dw_down, sums = mlp(
        attended, tokens, cotangent, rows, hidden_bias, first, second, third
    )
    sum_first, sum_in, sum_down, sum_vec, grad_tokens = back(
        lengths, q_heads, o_heads, lse, sums, d_att, kv, window, first,
        dw_out.reshape(2, 4, 4, 2, 3, 8, HALF), dw_in.reshape(2, *WIDE), dw_down.reshape(2, *TALL), d_one,
    )
    own = lax.dynamic_slice(sum_vec, (0, 6 * shard), (8, 6))
    own_in = lax.dynamic_slice(sum_vec[8:12].reshape(-1), (24 * shard,), (24,))
    return (
        layer_out, grad_tokens, sum_first[:, : 3 * width], own[0], own[1], sum_first[:, 3 * width :],
        own[2], own[3], own[4], sum_in, own_in, sum_down.reshape(24, width), own[5], own[6], own[7],
    )


def solution(mesh):
    both, own = P(("shard", "seq"), None), P("shard")
    rows = P("shard", None)
    return jax.shard_map(
        body,
        mesh=mesh,
        in_specs=(both, rows, own, own, rows, own, own, own, rows, own, rows, own, own, own, P(), both),
        out_specs=(both, both, rows, own, own, rows, own, own, own, rows, own, rows, own, own, own),
        check_vma=False,
    )
```

profile of v0, /device:TPU:1, one launch (start us, length us, event | category | flops | bytes accessed | tf_op | source)
XLA Modules:
  0.0 283.1 jit_solution(582588594094098462)
XLA Ops:
  0.6 0.8 maximum_bitcast_fusion
  1.4 1.5 pad_maximum_fusion.cat_ref
  2.9 0.8 stack.47
  3.7 0.7 pad_convert_fusion
  4.4 0.1 pad.11.clone
  4.5 0.7 maximum_maximum_fusion.vec_ref
  5.1 103.7 %front.1 = (bf16[2,2,2,4,4,2,3,8,384]{8,7,6,5,4,3,2,1,0:T(8,128)(2,1)}, bf16[2,2,2,4,4,2,3,8,384]{8,7,6,5,4,3,2,1,0:T(8,128)(2,1)}, bf16[2,4,4,2,2,2,3,8,384]{8,...) custom-call(s32[1,128]{1,0:T(1,128)} %bitcast.49, ...), custom_call_target="tpu_custom_call" | custom-call | tf_op jit(solution)/shard_map/front/pallas_call | solution.py:525
  108.8 27.3 %mlp.1 = (bf16[256,768]{1,0:T(8,128)(2,1)}, f32[256,768]{1,0:T(8,128)}, bf16[256,768]{1,0:T(8,128)(2,1)}, bf16[2,768,384]{2,1,0:T(8,128)(2,1)}, bf16[2,4,768,384...) custom-call(bf16[256,768]{1,0:T(8,128)(2,1)} %get-tuple-element.38.att_ref, ...), custom_call_target="tpu_custom_call" | custom-call | tf_op jit(solution)/shard_map/mlp/pallas_call | solution.py:1225
  136.1 136.4 %back.1 = (f32[6,3072]{1,0:T(8,128)}, f32[6,3072]{1,0:T(8,128)}, f32[3,8,768]{2,1,0:T(8,128)}, f32[16,768]{1,0:T(8,128)}, f32[256,768]{1,0:T(8,128)}) custom-call(s32[1,128]{1,0:T(1,128)} %bitcast.50, bf16[2,256,384]{2,1,0:T(8,128)(2,1)} %get-tuple-element.45.refs_1_, bf16[2,256,384]{2,1,0:T(8,128)(2,1)} %get-tuple-element.46.refs_2_, ...), custom_call_target="tpu_custom_call" | custom-call | tf_op jit(solution)/shard_map/back/pallas_call | solution.py:1061
  272.5 1.5 slice.33
  274.0 0.7 slice.40
  274.8 0.6 dynamic_slice.7
  275.3 1.3 slice.36
  276.7 0.8 constant_dynamic-slice_fusion
  277.5 0.5 slice_bitcast_fusion
  278.0 2.1 copy.34
  280.1 1.5 copy.35
  281.6 1.5 copy.36
  (3 shorter events, 0.0 us)
where the time goes:
time: 285 us; the launch traced here: 283 us
  Pallas kernels  267 us (94%)
  local copies, waits for them, and re-layouts  11.5 us (4%)
  other arithmetic  3.59 us (1%)
    pallas_call x1, Pallas kernels, back(): pl.pallas_call(back_kernel, name='back', out_shape=(jax.ShapeDtypeStruct(...  136 us
    pallas_call x1, Pallas kernels, front(): pl.pallas_call(front_kernel, name='front', out_shape=(jax.ShapeDtypeStruc...  104 us
    pallas_call x1, Pallas kernels, mlp(): pl.pallas_call(mlp_kernel, name='mlp', in_specs=[IN_VMEM] * 5 + [ANY_SPAC...  27.3 us

commit v1 on v0

--- a/solution.py
+++ b/solution.py
@@ -1139,8 +1139,8 @@
 
 def mlp_kernel(
     att_ref, tok_ref, cot_ref, rows, bias_in, first, second, third,
-    out_ref, d_one_ref, d_att_ref, dwo_ref, dw_in_ref, dw_down_ref, sums_ref,
-    w_out, w_in, w_down, n_one, low, low_flip, slope, active, wide, sem,
+    out_ref, d_one_ref, d_att_ref, dwo_ref, dw_in_out, dw_down_out, sums_ref,
+    dw_in_ref, dw_down_ref, out_sem,    w_out, w_in, w_down, n_one, low, low_flip, slope, active, wide, sem,
 ):
     f32, bf = jnp.float32, jnp.bfloat16
     loads = [pltpu.make_async_copy(first.at[:, 3], w_out, sem.at[0])]
@@ -1198,7 +1198,22 @@
         d_hidden = (d_active * slope[m]).astype(bf)
         sums_ref[pl.ds(8 + m // 2, 1), pl.ds(pl.multiple_of(lax.rem(m, 2) * HALF, 128), HALF)] = row_sum(d_hidden.astype(f32))
         dw_in_ref[lax.rem(m, 2), m // 2] = dot32(low_flip[...], d_hidden).astype(bf)
+        for cp in leaving(m):
+            cp.start()
         wide[...] += across_lanes(d_hidden, w_in[lax.rem(m, 2), m // 2])
+        return carry
+
+    def leaving(m):
+        piece = lax.rem(m, 2), m // 2
+        return [
+            pltpu.make_async_copy(dw_in_ref.at[piece], dw_in_out.at[piece], out_sem.at[m, 0]),
+            pltpu.make_async_copy(dw_down_ref.at[0, m], dw_down_out.at[0, m], out_sem.at[m, 1]),
+            pltpu.make_async_copy(dw_down_ref.at[1, m], dw_down_out.at[1, m], out_sem.at[m, 2]),
+        ]
+
+    def left(m, carry):
+        for cp in leaving(m):
+            cp.wait()
         return carry
 
     lax.fori_loop(0, 8, down, 0)
@@ -1218,6 +1233,7 @@
         part = across_lanes(d_half, w_out[h])
         d_att = part if d_att is None else d_att + part
     d_att_ref[...] = d_att.astype(bf)
+    lax.fori_loop(0, 8, left, 0)
 
 
 def mlp(att, tokens, cotangent, rows, bias_in, first, second, third):
@@ -1226,7 +1242,7 @@
         mlp_kernel,
         name="mlp",
         in_specs=[IN_VMEM] * 5 + [ANY_SPACE] * 3,
-        out_specs=(IN_VMEM,) * 7,
+        out_specs=(IN_VMEM,) * 4 + (ANY_SPACE,) * 2 + (IN_VMEM,),
         out_shape=(
             jax.ShapeDtypeStruct((TILE, 768), bf),
             jax.ShapeDtypeStruct((TILE, 768), f32),
@@ -1237,6 +1253,9 @@
             jax.ShapeDtypeStruct((16, 768), f32),
         ),
         scratch_shapes=[
+            pltpu.VMEM((2, 4, 768, HALF), bf),
+            pltpu.VMEM((2, 8, HALF, HALF), bf),
+            pltpu.SemaphoreType.DMA((8, 3)),
             pltpu.VMEM((2, 768, HALF), bf),
             pltpu.VMEM((2, 4, 768, HALF), bf),
             pltpu.VMEM((2, 8, HALF, HALF), bf),

time: 285 us -> 283 us (level)
  no operation moved by 1% of the time
where the time goes in v1:
time: 283 us; the launch traced here: 282 us
  Pallas kernels  266 us (94%)
  local copies, waits for them, and re-layouts  11.5 us (4%)
  other arithmetic  3.59 us (1%)
    pallas_call x1, Pallas kernels, back(): pl.pallas_call(back_kernel, name='back', out_shape=(jax.ShapeDtypeStruct(...  137 us
    pallas_call x1, Pallas kernels, front(): pl.pallas_call(front_kernel, name='front', out_shape=(jax.ShapeDtypeStruc...  104 us
    pallas_call x1, Pallas kernels, mlp(): pl.pallas_call(mlp_kernel, name='mlp', in_specs=[IN_VMEM] * 5 + [ANY_SPAC...  25.6 us

profile of v1, /device:TPU:1, one launch (start us, length us, event | category | flops | bytes accessed | tf_op | source)
XLA Modules:
  0.0 282.2 jit_solution(8348086959949541609)
XLA Ops:
  0.6 0.8 maximum_bitcast_fusion
  1.4 1.5 pad_maximum_fusion.cat_ref
  2.9 0.8 stack.47
  3.7 0.7 pad_convert_fusion
  4.4 0.1 pad.11.clone
  4.5 0.7 maximum_maximum_fusion.vec_ref
  5.1 103.7 %front.1 = (bf16[2,2,2,4,4,2,3,8,384]{8,7,6,5,4,3,2,1,0:T(8,128)(2,1)}, bf16[2,2,2,4,4,2,3,8,384]{8,7,6,5,4,3,2,1,0:T(8,128)(2,1)}, bf16[2,4,4,2,2,2,3,8,384]{8,...) custom-call(s32[1,128]{1,0:T(1,128)} %bitcast.49, ...), custom_call_target="tpu_custom_call" | custom-call | tf_op jit(solution)/shard_map/front/pallas_call | solution.py:525
  108.8 25.6 %mlp.1 = (bf16[256,768]{1,0:T(8,128)(2,1)}, f32[256,768]{1,0:T(8,128)}, bf16[256,768]{1,0:T(8,128)(2,1)}, bf16[2,768,384]{2,1,0:T(8,128)(2,1)}, bf16[2,4,768,384...) custom-call(bf16[256,768]{1,0:T(8,128)(2,1)} %get-tuple-element.38.att_ref, ...), custom_call_target="tpu_custom_call" | custom-call | tf_op jit(solution)/shard_map/mlp/pallas_call | solution.py:1241
  134.4 137.1 %back.1 = (f32[6,3072]{1,0:T(8,128)}, f32[6,3072]{1,0:T(8,128)}, f32[3,8,768]{2,1,0:T(8,128)}, f32[16,768]{1,0:T(8,128)}, f32[256,768]{1,0:T(8,128)}) custom-call(s32[1,128]{1,0:T(1,128)} %bitcast.50, bf16[2,256,384]{2,1,0:T(8,128)(2,1)} %get-tuple-element.45.refs_1_, bf16[2,256,384]{2,1,0:T(8,128)(2,1)} %get-tuple-element.46.refs_2_, ...), custom_call_target="tpu_custom_call" | custom-call | tf_op jit(solution)/shard_map/back/pallas_call | solution.py:1061
  271.6 1.5 slice.33
  273.1 0.7 slice.40
  273.9 0.6 dynamic_slice.7
  274.4 1.3 slice.36
  275.8 0.8 constant_dynamic-slice_fusion
  276.6 0.5 slice_bitcast_fusion
  277.1 2.1 copy.34
  279.2 1.5 copy.35
  280.7 1.5 copy.36
  (3 shorter events, 0.0 us)
